TPU v7x, 32 devices: a whole 2x2x4 slice. The times are simulated.
32 devices in a mesh: doc: 4 (over z), seq: 8 (over y, x, core).
Axes of the slice: x: 2, y: 2, z: 4, core: 2. Of those that a mesh axis runs over, the one named last changes fastest.
Arguments:
- features: bfloat16 [4096, 1280], P(('doc', 'seq')), parts along dimension 0, may hold values from -6 to 6
- gate_in: bfloat16 [4096, 1024], P(('doc', 'seq')), parts along dimension 0, may hold values from -6 to 6
- conv_weight: float32 [4, 1280], replicated, may hold values from -3 to 3
- conv_bias: float32 [1280], replicated, may hold values from -0.5 to 0.5
- log_decay: float32 [4096, 16], P(('doc', 'seq')), parts along dimension 0, may hold values from -0.6 to 0
- step_size: float32 [4096, 16], P(('doc', 'seq')), parts along dimension 0, may hold values from 0 to 2
- gate_gain: float32 [1024], replicated, may hold values from 0.25 to 1.75
- w_out: bfloat16 [1024, 1024], replicated, may hold values from -0.1875 to 0.1875
- boundaries: int32 [1024], P('doc'), parts along dimension 0, may hold values from 0 to 1023, as said below
- pad_vector: bfloat16 [512], replicated, may hold values from -5 to 5
- main_gain: float32 [1536], replicated, may hold values from 0.25 to 1.75
- w_gate: bfloat16 [1536, 4096], P(None, 'seq'), may hold values from -0.15625 to 0.15625
- w_up: bfloat16 [1536, 4096], P(None, 'seq'), may hold values from -0.15625 to 0.15625
- w_down: bfloat16 [4096, 1024], P('seq'), may hold values from -0.09375 to 0.09375
Outputs:
- byte_out: bfloat16 [4096, 1024], P(('doc', 'seq')), parts along dimension 0
There are 4 independent parts, one for each index of `doc`. A program takes and returns all parts, laid end to end along the dimension named above; an argument that names none is the same for every part. Nothing has to cross between parts.
Inputs may be any that keep to these rules, and one draw needn't show every extreme that they name: Strictly increasing, boundaries[0] = 0. For every k = 1, 2, ..., the number of entries below k * 128 lies between k * 32 and k * 32 + 31, and the upper end is reached at some k in every draw. The bytes of one device hold 1 to 63 entries, and some device holds exactly 63.
All inputs are finite; a program needn't handle non-finite values.
Results may differ from a plain program's by a relative error of at most 0.02.
Values may be sent and summed in bfloat16 or wider, within the bound.
A program may use at most 64 MiB of HBM per device.

v0:
```python
import jax
import jax.numpy as jnp
from jax import lax
from jax.sharding import PartitionSpec as P

EPSILON = 1e-05


def shifted(value, axis, by):
    size = lax.axis_size(axis)
    pairs = [(i, i + by) for i in range(size) if 0 <= i + by < size]
    return lax.ppermute(value, axis, pairs)


def prefix(value, axis, combine, identity):
    size, index = (lax.axis_size(axis), lax.axis_index(axis))
    everything = jax.tree.map(
        lambda part, kind: lax.all_gather(part.astype(kind), axis),
        value,
        (jnp.bfloat16, jnp.bfloat16),
    )
    start = jax.tree.map(
        lambda part, zero: jnp.broadcast_to(jnp.asarray(zero, part.dtype), part.shape),
        value,
        identity,
    )

    def step(k, before):
        reached = k < index
        new = combine(
            before, jax.tree.map(lambda part, own: part[k].astype(own.dtype), everything, value)
        )
        return jax.tree.map(lambda a, b: jnp.where(reached, a, b), new, before)

    return lax.fori_loop(0, size, step, start)


def rms_scale(values):
    return values * lax.rsqrt(jnp.mean(values * values, axis=-1, keepdims=True) + EPSILON)


def join_states(earlier, latter):
    return (earlier[0] * latter[0], latter[0][:, None, None] * earlier[1] + latter[1])


def main_section(block_rows, pad_vector, main_gain, w_gate, w_up, w_down):
    fragment = lax.all_gather(block_rows, "seq", axis=0, tiled=True)
    filler = jnp.broadcast_to(pad_vector[None, :], (fragment.shape[0], pad_vector.shape[0]))
    joined = jnp.concatenate([fragment, filler], 1).astype(jnp.float32)
    normed = (rms_scale(joined) * main_gain).astype(jnp.bfloat16)
    gate_part = jnp.dot(normed, w_gate, preferred_element_type=jnp.float32)
    up_part = jnp.dot(normed, w_up, preferred_element_type=jnp.float32)
    activated = (jax.nn.silu(gate_part) * up_part).astype(jnp.bfloat16)
    summed = lax.psum_scatter(
        jnp.dot(activated, w_down, preferred_element_type=jnp.float32).astype(jnp.bfloat16),
        "seq",
        scatter_dimension=0,
        tiled=True,
    ).astype(jnp.float32)
    return (block_rows.astype(jnp.float32) + summed).astype(jnp.bfloat16)


def per_device(
    features,
    gate_in,
    conv_weight,
    conv_bias,
    log_decay,
    step_size,
    gate_gain,
    w_out,
    boundaries,
    pad_vector,
    main_gain,
    w_gate,
    w_up,
    w_down,
):
    rows_dev = features.shape[0]
    kernel_width = conv_weight.shape[0]
    rim_rows = shifted(features[rows_dev - kernel_width + 1 :], "seq", 1)
    padded = jnp.concatenate([rim_rows, features], 0)
    conv_mixed = conv_bias[None, :] + jnp.zeros((rows_dev, features.shape[1]), jnp.float32)
    for tap_index in range(kernel_width):
        conv_mixed = conv_mixed + conv_weight[tap_index][None, :] * padded[
            tap_index : tap_index + rows_dev
        ].astype(jnp.float32)
    conv_mixed = jax.nn.silu(conv_mixed).astype(jnp.bfloat16)
    head_count = log_decay.shape[1]
    inner_width = gate_in.shape[1]
    head_dim = inner_width // head_count
    state_dim = (features.shape[1] - inner_width) // 2
    x_part = conv_mixed[:, :inner_width]
    b_part = conv_mixed[:, inner_width : inner_width + state_dim]
    c_part = conv_mixed[:, inner_width + state_dim :]
    cumulative = jnp.cumsum(log_decay, axis=0).T
    total_decay = cumulative[:, -1]
    inner_prod = jnp.dot(c_part, b_part.T, preferred_element_type=jnp.float32)
    row_ids = lax.iota(jnp.int32, rows_dev)
    causal = row_ids[:, None] >= row_ids[None, :]
    decay_gaps = jnp.where(causal[None], cumulative[:, :, None] - cumulative[:, None, :], -jnp.inf)
    mix_weights = jnp.exp(decay_gaps) * inner_prod[None] * step_size.T[:, None, :]
    x_heads = x_part.reshape(rows_dev, head_count, head_dim)
    local_out = jnp.einsum("hts,shp->thp", mix_weights, x_heads, preferred_element_type=jnp.float32)
    end_coef = jnp.exp(total_decay[:, None] - cumulative) * step_size.T
    local_state = jnp.einsum(
        "hs,shp,sn->hpn", end_coef, x_heads, b_part, preferred_element_type=jnp.float32
    )
    decay_in, state_in = prefix(
        (jnp.exp(total_decay), local_state),
        "seq",
        join_states,
        (jnp.ones_like(total_decay), jnp.zeros_like(local_state)),
    )
    carried = (
        jnp.einsum("tn,hpn->thp", c_part, state_in, preferred_element_type=jnp.float32)
        * jnp.exp(cumulative.T)[:, :, None]
    )
    ssm_out = (local_out + carried).reshape(rows_dev, inner_width)
    gated_out = ssm_out * jax.nn.silu(gate_in.astype(jnp.float32))
    normed = (rms_scale(gated_out) * gate_gain).astype(jnp.bfloat16)
    encoded = jnp.dot(normed, w_out, preferred_element_type=jnp.float32).astype(jnp.bfloat16)
    dev_index = lax.axis_index("seq")
    seq_count = lax.axis_size("seq")
    per_owner = boundaries.shape[0] // seq_count
    slot_count = 2 * per_owner
    first_byte = dev_index * rows_dev
    positions = first_byte + row_ids
    block_of = jnp.sum((boundaries[:, None] <= positions[None, :]).astype(jnp.int32), axis=0) - 1
    is_start = jnp.any(boundaries[:, None] == positions[None, :], axis=0)
    slot_ids = lax.iota(jnp.int32, slot_count)
    base_block = dev_index * per_owner
    slot_of = block_of - base_block
    pick_matrix = ((slot_of[None, :] == slot_ids[:, None]) & is_start[None, :]).astype(jnp.bfloat16)
    picked = jnp.dot(pick_matrix, encoded, preferred_element_type=jnp.float32).astype(jnp.bfloat16)
    arriving = shifted(picked[per_owner:], "seq", 1)
    owned_rows = picked[:per_owner] + arriving
    results = main_section(owned_rows, pad_vector, main_gain, w_gate, w_up, w_down)
    following = shifted(results, "seq", -1)
    out_table = jnp.concatenate([results, following], 0)
    last_row = results[per_owner - 1 :]
    earlier_row = shifted(last_row, "seq", 1)
    spread = (slot_of[:, None] == slot_ids[None, :]).astype(jnp.bfloat16)
    expanded = jnp.dot(spread, out_table, preferred_element_type=jnp.float32)
    expanded = expanded + jnp.where((slot_of == -1)[:, None], earlier_row.astype(jnp.float32), 0.0)
    return (encoded.astype(jnp.float32) + expanded).astype(jnp.bfloat16)


def solution(mesh):
    in_specs = (
        P(("doc", "seq"), None),
        P(("doc", "seq"), None),
        P(),
        P(),
        P(("doc", "seq"), None),
        P(("doc", "seq"), None),
        P(),
        P(),
        P("doc"),
        P(),
        P(),
        P(None, "seq"),
        P(None, "seq"),
        P("seq", None),
    )
    out_specs = P(("doc", "seq"), None)
    return jax.shard_map(
        per_device, mesh=mesh, in_specs=in_specs, out_specs=out_specs, check_vma=False
    )
```

profile of v0, /device:TPU:1, one launch (start us, length us, event | category | flops | bytes accessed | tf_op | source)
XLA Modules:
  0.0 128.0 jit_solution(9124794253059897959)
XLA Ops:
  6.5 0.9 slice.46
  7.4 4.5 %collective-permute-start = (bf16[3,1280]{1,0:T(4,128)(2,1)S(1)}, bf16[3,1280]{1,0:T(4,128)(2,1)S(1)}, u32[]{:S(2)}, u32[]{:S(2)}) collective-permute-start(bf16[3,1280]{1,0:T(4,128)(2,1)S(1)} %slice.46), channel_id=1, source_target_pairs={{0,1},{1,2},{2,3},{3,4},{4,5},{5,6},{6,7},{8,9},{9,10},{10,11},{11... | collective-permute-start | bytes 23048 | tf_op jit(solution)/shard_map/ppermute | solution.py:12
  11.9 0.8 copy.34
  12.9 0.8 copy.37
  13.7 0.9 slice_reduce_fusion.3
  14.7 2.1 %multiply_convert_fusion = bf16[128,1280]{1,0:T(8,128)(2,1)S(1)} fusion(bf16[128,1280]{1,0:T(8,128)(2,1)} %param.16, bf16[3,1280]{1,0:T(4,128)(2,1)S(1)} %collective-permute-done, f32[1280]{0:T(1024)S(1)} %get-tuple-element.120, f32[1280]{0:T(1024)S(1)} %get-tuple-element.121, f32[1280]{0:T(1024)S(1)} %get-tuple-element.119, ...), kind=kLoop, calls=%fused_computation.28 | loop fusion | flops 4259840 | bytes 688640 | tf_op jit(solution)/shard_map/convert_element_type | solution.py:88
  17.0 0.9 convolution_convert_fusion.2
  18.1 0.7 copy.35
  18.8 0.6 dynamic-slice
  20.2 10.3 %all-reduce = bf16[128]{0:T(256)(128)(2,1)S(1)} all-reduce(bf16[128]{0:T(256)(128)(2,1)S(1)} %dynamic-update-slice), channel_id=2, replica_groups=mesh['doc'=4,'seq'=8] {'seq'}, use_global_device_ids=true, to_apply=%add | all-reduce | flops 128 | bytes 512
  30.9 0.6 compare_reduce_fusion
  32.2 14.0 %all-gather.4.cloned.1.call-done = bf16[128,64,128]{2,1,0:T(8,128)(2,1)} async-done(((bf16[16,64,128]{2,1,0:T(8,128)(2,1)}), bf16[128,64,128]{2,1,0:T(8,128)(2,1)}) %all-gather.4.cloned.1.call-update) | async-done | bytes 2097168 | tf_op jit(solution)/shard_map/all_gather | solution.py:18
  46.2 9.0 %while.14 = (s32[]{:T(128)}, f32[16,64,128]{2,1,0:T(8,128)S(1)}, s32[]{:T(128)}, bf16[8,16]{1,0:T(8,128)(2,1)S(1)}, bf16[8,16,64,128]{3,2,1,0:T(8,128)(2,1)}, /*index=5*/s32[]{:T(128)}, s32[]{:T(128)}) while((s32[]{:T(128)}, f32[16,64,128]{2,1,0:T(8,128)S(1)}, s32[]{:T(128)}, bf16[8,16]{1,0:T(8,128)(2,1)S(1)}, ...), condition=%wide.region_2.3_spmd.clone, body=%wide.region_1.2_spmd.clone.sunk | while | flops 655380 | bytes 1310985 | solution.py:35
  46.2 1.1 fusion.71
  47.3 1.1 fusion.71
  48.4 1.1 fusion.71
  49.6 1.1 fusion.71
  50.7 1.1 fusion.71
  51.8 1.1 fusion.71
  53.0 1.1 fusion.71
  54.1 1.1 fusion.71
  55.4 1.3 %fusion.4 = f32[128,16,64]{0,2,1:T(8,128)S(1)} fusion(f32[128,16,64]{0,2,1:T(8,128)S(1)} %convolution_multiply_fusion.1, bf16[128,16,64]{0,2,1:T(8,128)(2,1)S(1)} %bitcast.48, f32[16,128]{1,0:T(8,128)} %bitcast.51, f32[128,128]{1,0:T(8,128)S(1)} %fusion.50, f32[16,128]{1,0:T(8,128)} %copy.35, pred[128,128]{1,0:T(8,128)(4,1)S(1)} %iota_compare_fusion.1), kind=kOutput, calls=%fused_computation.11 | convolution fusion | flops 34734080 | bytes 1409024 | tf_op jit(solution)/shard_map/hts,shp->thp/dot_general | solution.py:104
  58.3 3.4 %collective-permute-start.1 = (bf16[32,1024]{1,0:T(8,128)(2,1)S(1)}, bf16[32,1024]{1,0:T(8,128)(2,1)S(1)}, u32[]{:S(2)}, u32[]{:S(2)}) collective-permute-start(bf16[32,1024]{1,0:T(8,128)(2,1)S(1)} %slice.69), channel_id=1, source_target_pairs={{0,1},{1,2},{2,3},{3,4},{4,5},{5,6},{6,7},{8,9},{9,10},{10,11},{11... | collective-permute-start | bytes 196616 | tf_op jit(solution)/shard_map/ppermute | solution.py:12
  61.7 1.3 %collective-permute-done.1 = bf16[32,1024]{1,0:T(8,128)(2,1)S(1)} collective-permute-done((bf16[32,1024]{1,0:T(8,128)(2,1)S(1)}, bf16[32,1024]{1,0:T(8,128)(2,1)S(1)}, u32[]{:S(2)}, u32[]{:S(2)}) %collective-permute-start.1) | collective-permute-done | bytes 65568 | tf_op jit(solution)/shard_map/ppermute | solution.py:12
  63.0 11.8 %all_gather.16 = bf16[256,1024]{1,0:T(8,128)(2,1)S(1)} all-gather(bf16[32,1024]{1,0:T(8,128)(2,1)S(1)} %slice_add_fusion), channel_id=1, replica_groups=mesh['doc'=4,'seq'=8] {'seq'}, dimensions={0}, use_global_device_ids=true | all-gather | bytes 589824 | tf_op jit(solution)/shard_map/all_gather | solution.py:47
  75.7 3.5 %convolution_convert_fusion = bf16[256,1024]{1,0:T(8,128)(2,1)} fusion(bf16[512,1024]{1,0:T(8,128)(2,1)} %param.29, bf16[1536,512]{1,0:T(8,128)(2,1)} %param.28, f32[256,512]{1,0:T(8,128)S(1)} %fusion.38, f32[1536]{0:T(1024)S(1)} %copy-done.8, f32[256]{0:T(256)S(1)} %add_rsqrt_fusion, bf16[256,1024]{1,0:T(8,128)(2,1)S(1)} %all_gather.16, ...), kind=kOutput, calls=%fused_computation.8 | convolution fusion | flops 674889728 | bytes 4204544 | tf_op jit(solution)/shard_map/dot_general | solution.py:55
  79.3 33.2 %reduce-scatter.2.cloned.1.call-done = bf16[32,1024]{1,0:T(8,128)(2,1)} async-done(((bf16[256,1024]{1,0:T(8,128)(2,1)}), bf16[32,1024]{1,0:T(8,128)(2,1)}) %reduce-scatter.2.cloned.1.call-update) | async-done | bytes 65552 | tf_op jit(solution)/shard_map/reduce_scatter | solution.py:54
  112.4 0.9 add_convert_fusion
  113.3 3.1 %collective-permute-start.2 = (bf16[32,1024]{1,0:T(8,128)(2,1)S(1)}, bf16[32,1024]{1,0:T(8,128)(2,1)S(1)}, u32[]{:S(2)}, u32[]{:S(2)}) collective-permute-start(bf16[32,1024]{1,0:T(8,128)(2,1)S(1)} %add_convert_fusion), channel_id=1, source_target_pairs={{1,0},{2,1},{3,2},{4,3},{5,4},{6,5},{7,6},{9,8},{10,9},{11,10},{12... | collective-permute-start | bytes 196616 | tf_op jit(solution)/shard_map/ppermute | solution.py:12
  116.5 3.0 %collective-permute-start.3 = (bf16[1,1024]{1,0:T(2,128)(2,1)S(1)}, bf16[1,1024]{1,0:T(2,128)(2,1)S(1)}, u32[]{:S(2)}, u32[]{:S(2)}) collective-permute-start(bf16[1,1024]{1,0:T(2,128)(2,1)S(1)} %slice.70), channel_id=1, source_target_pairs={{0,1},{1,2},{2,3},{3,4},{4,5},{5,6},{6,7},{8,9},{9,10},{10,11},{11... | collective-permute-start | bytes 6152 | tf_op jit(solution)/shard_map/ppermute | solution.py:12
  119.5 0.7 collective-permute-done.3
  120.2 1.0 fusion.6
  (67 shorter events, 4.4 us)
Async XLA Ops:
  6.5 50.7 %copy-start = (bf16[1024,1024]{1,0:T(8,128)(2,1)S(1)}, bf16[1024,1024]{1,0:T(8,128)(2,1)}, u32[]{:S(2)}) copy-start(bf16[1024,1024]{1,0:T(8,128)(2,1)} %param.23) | copy-start | bytes 6291460
  6.5 39.6 %all-gather.4.cloned.1.call-start = ((), (), s32[]{:S(2)}) async-start(), calls=%async_computation.2 | async-start | bytes 2359296 | tf_op jit(solution)/shard_map/all_gather | solution.py:18
  7.4 7.3 %collective-permute-start = (bf16[3,1280]{1,0:T(4,128)(2,1)S(1)}, bf16[3,1280]{1,0:T(4,128)(2,1)S(1)}, u32[]{:S(2)}, u32[]{:S(2)}) collective-permute-start(bf16[3,1280]{1,0:T(4,128)(2,1)S(1)} %slice.46), channel_id=1, source_target_pairs={{0,1},{1,2},{2,3},{3,4},{4,5},{5,6},{6,7},{8,9},{9,10},{10,11},{11... | collective-permute-start | bytes 23048 | tf_op jit(solution)/shard_map/ppermute | solution.py:12
  13.7 5.1 %copy-start.10 = (u32[32]{0:T(128)S(1)}, u32[32]{0:T(128)}, u32[]{:S(2)}) copy-start(u32[32]{0:T(128)} %constant.64) | copy-start | bytes 388
  13.7 17.0 %copy-start.2 = (s32[256]{0:T(256)S(1)}, s32[256]{0:T(256)}, u32[]{:S(2)}) copy-start(s32[256]{0:T(256)} %param.24) | copy-start | bytes 3076
  18.0 94.4 %reduce-scatter.2.cloned.1.call-start = ((), (), s32[]{:S(2)}) async-start(), calls=%async_computation.1 | async-start | bytes 589824 | tf_op jit(solution)/shard_map/reduce_scatter | solution.py:54
  55.4 1.6 %copy-start.1 = (bf16[128,1024]{1,0:T(8,128)(2,1)S(1)}, bf16[128,1024]{1,0:T(8,128)(2,1)}, u32[]{:S(2)}) copy-start(bf16[128,1024]{1,0:T(8,128)(2,1)} %param.17) | copy-start | bytes 786436
  56.8 0.7 copy-start.9
  57.5 0.6 copy-start.3
  57.5 0.6 copy-start.4
  57.5 4.3 %copy-start.5 = (bf16[512]{0:T(512)(128)(2,1)S(1)}, bf16[512]{0:T(512)(128)(2,1)}, u32[]{:S(2)}) copy-start(bf16[512]{0:T(512)(128)(2,1)} %param.25) | copy-start | bytes 3076
  58.1 17.0 %copy-start.7 = (bf16[1536,512]{1,0:T(8,128)(2,1)S(1)}, bf16[1536,512]{1,0:T(8,128)(2,1)}, u32[]{:S(2)}) copy-start(bf16[1536,512]{1,0:T(8,128)(2,1)} %param.27) | copy-start | bytes 4718596
  58.1 17.0 %copy-start.8 = (f32[1536]{0:T(1024)S(1)}, f32[1536]{0:T(1024)}, u32[]{:S(2)}) copy-start(f32[1536]{0:T(1024)} %param.26) | copy-start | bytes 18436
  58.3 4.7 %collective-permute-start.1 = (bf16[32,1024]{1,0:T(8,128)(2,1)S(1)}, bf16[32,1024]{1,0:T(8,128)(2,1)S(1)}, u32[]{:S(2)}, u32[]{:S(2)}) collective-permute-start(bf16[32,1024]{1,0:T(8,128)(2,1)S(1)} %slice.69), channel_id=1, source_target_pairs={{0,1},{1,2},{2,3},{3,4},{4,5},{5,6},{6,7},{8,9},{9,10},{10,11},{11... | collective-permute-start | bytes 196616 | tf_op jit(solution)/shard_map/ppermute | solution.py:12
  75.7 44.5 %copy-start.6 = (pred[128]{0:T(512)(128)(4,1)S(1)}, pred[128]{0:T(512)(128)(4,1)}, u32[]{:S(2)}) copy-start(pred[128]{0:T(512)(128)(4,1)} %get-tuple-element.132) | copy-start | bytes 388
  113.3 6.9 %collective-permute-start.2 = (bf16[32,1024]{1,0:T(8,128)(2,1)S(1)}, bf16[32,1024]{1,0:T(8,128)(2,1)S(1)}, u32[]{:S(2)}, u32[]{:S(2)}) collective-permute-start(bf16[32,1024]{1,0:T(8,128)(2,1)S(1)} %add_convert_fusion), channel_id=1, source_target_pairs={{1,0},{2,1},{3,2},{4,3},{5,4},{6,5},{7,6},{9,8},{10,9},{11,10},{12... | collective-permute-start | bytes 196616 | tf_op jit(solution)/shard_map/ppermute | solution.py:12
  116.5 3.7 %collective-permute-start.3 = (bf16[1,1024]{1,0:T(2,128)(2,1)S(1)}, bf16[1,1024]{1,0:T(2,128)(2,1)S(1)}, u32[]{:S(2)}, u32[]{:S(2)}) collective-permute-start(bf16[1,1024]{1,0:T(2,128)(2,1)S(1)} %slice.70), channel_id=1, source_target_pairs={{0,1},{1,2},{2,3},{3,4},{4,5},{5,6},{6,7},{8,9},{9,10},{10,11},{11... | collective-permute-start | bytes 6152 | tf_op jit(solution)/shard_map/ppermute | solution.py:12
Sparse Core Ops, SparseCore 0:
  18.1 27.9 all-gather.3
  79.4 33.0 reduce-scatter.1
where the time goes:
time: 130 us; the launch traced here: 128 us
  waiting for transfers between devices  49.2 us (38%)
  blocking collectives  22.1 us (17%)
  between operations  14.3 us (11%)
  starting transfers between devices  14.1 us (11%)
  other arithmetic  13.8 us (11%)
  matrix products  8.49 us (7%)
  local copies, waits for them, and re-layouts  5.81 us (4%)
    reduce_scatter x1, waiting for transfers between devices, main_section(): lax.psum_scatter(jnp.dot(activated, w_down, preferred_element_type=jnp.fl...  33.2 us
    ppermute x4, starting transfers between devices, shifted(): return lax.ppermute(value, axis, pairs)  14 us
    all_gather x1, waiting for transfers between devices, prefix(): lax.all_gather(part.astype(kind), axis)  14 us
    all_gather x1, blocking collectives, main_section(): fragment = lax.all_gather(block_rows, 'seq', axis=0, tiled=True)  11.8 us
    unnamed x1, blocking collectives  10.3 us
    select_n x8, other arithmetic, step(): return jax.tree.map(lambda a, b: jnp.where(reached, a, b), new, before)  8.73 us
    dot_general x1, matrix products, main_section(): jnp.dot(activated, w_down, preferred_element_type=jnp.float32)  3.53 us
    unnamed x27, local copies, waits for them, and re-layouts  2.71 us
  transfers between devices with their start and end apart: 6, of which 4 were waited for; matrix products, arithmetic and copies ran while one was open for 5% of the time, Pallas kernels for 0%

commit v1 on v0

v1 whole, which is shorter than its diff:
```python
import functools

import jax
import jax.numpy as jnp
from jax import lax
from jax.experimental import pallas as pl
from jax.experimental.pallas import tpu as pltpu
from jax.sharding import PartitionSpec as P

EPSILON = 1e-05
TILE = 16
F32 = jnp.float32
BF16 = jnp.bfloat16


def mm(a, b):
    return jnp.dot(a, b, preferred_element_type=F32)


def silu(v):
    return v / (1.0 + jnp.exp(-v))


def kernel(
    n,
    features,
    gate_hbm,
    conv_weight,
    conv_bias,
    log_decay,
    step_size,
    gate_gain,
    w_out_hbm,
    boundaries,
    pad_vector,
    main_gain,
    w_gate_hbm,
    w_up_hbm,
    w_down_hbm,
    out,
    gate_in,
    w_out,
    w_gate,
    w_up,
    w_down,
    halo,
    xs,
    dec,
    sbuf,
    rbuf,
    obuf,
    inbuf,
    enc,
    upper,
    arrived,
    gath,
    nbuf,
    part,
    pair,
    csend,
    crecv,
    table,
    load_sem,
    one_send,
    one_recv,
    dec_send,
    dec_recv,
    st1_send,
    st1_recv,
    st2_send,
    st2_recv,
    ag_send,
    fwd_send,
    ag_recv,
    pair_send,
    pair_recv,
    chip_send,
    chip_recv,
):
    me = lax.axis_index("seq")
    chips = n // 2
    chip, core = lax.div(me, 2), lax.rem(me, 2)
    partner = chip * 2 + (1 - core)
    nxt, prv = lax.rem(me + 1, n), lax.rem(me + n - 1, n)
    rows, channels = features.shape
    heads = log_decay.shape[1]
    inner = gate_in.shape[1]
    head_dim = inner // heads
    state_dim = (channels - inner) // 2
    piece = state_dim // n
    per = gath.shape[1]
    taps = conv_weight.shape[0]

    barrier = pltpu.get_barrier_semaphore()
    for off in range(1, n):
        pl.semaphore_signal(
            barrier,
            inc=1,
            device_id={"seq": lax.rem(me + off, n)},
            device_id_type=pl.DeviceIdType.MESH,
        )

    loads = []
    for i, (src, dst) in enumerate(
        (
            (gate_hbm, gate_in),
            (w_out_hbm, w_out),
            (w_gate_hbm, w_gate),
            (w_up_hbm, w_up),
            (w_down_hbm, w_down),
        )
    ):
        c = pltpu.make_async_copy(src, dst, load_sem.at[i])
        c.start()
        loads.append(c)

    def remote(src, dst, ssem, rsem, peer):
        return pltpu.make_async_remote_copy(
            src_ref=src,
            dst_ref=dst,
            send_sem=ssem,
            recv_sem=rsem,
            device_id={"seq": peer},
            device_id_type=pl.DeviceIdType.MESH,
        )

    row_i = lax.broadcasted_iota(jnp.int32, (rows, rows), 0)
    col_i = lax.broadcasted_iota(jnp.int32, (rows, rows), 1)
    causal = row_i >= col_i
    cum = jnp.dot(
        causal.astype(F32),
        log_decay[...],
        preferred_element_type=F32,
        precision=lax.Precision.HIGHEST,
    )
    total = cum[rows - 1 :, :]
    mid = cum[rows // 2 : rows // 2 + 1, :]
    dec[me] = jnp.zeros(dec.shape[1:], F32)
    dec[me, :, :heads] = jnp.broadcast_to(total, (dec.shape[1], heads))

    pl.semaphore_wait(barrier, n - 1)

    halo_copy = remote(
        features.at[pl.ds(rows - TILE, TILE)], halo, one_send.at[0], one_recv.at[0], nxt
    )
    halo_copy.start()
    dec_copies = []
    for off in range(1, n):
        peer = lax.rem(me + off, n)
        c = remote(dec.at[me], dec.at[me], dec_send.at[peer], dec_recv.at[me], peer)
        c.start()
        dec_copies.append(c)

    hid = lax.broadcasted_iota(jnp.int32, (heads, inner), 0) * head_dim
    lane = lax.broadcasted_iota(jnp.int32, (heads, inner), 1)
    onehot = ((lane >= hid) & (lane < hid + head_dim)).astype(F32).astype(BF16)

    def expand(v):
        hi = v.astype(BF16)
        lo = (v - hi.astype(F32)).astype(BF16)
        return mm(hi, onehot) + mm(lo, onehot)

    in_coef = expand(step_size[...] * jnp.exp(mid - cum))
    out_coef = expand(jnp.exp(cum - mid))
    mid_to_end = expand(jnp.broadcast_to(jnp.exp(total - mid), (8, heads)))[:1]
    start_to_mid = expand(jnp.broadcast_to(jnp.exp(mid), (8, heads)))[:1]

    xs[pl.ds(TILE, rows), :] = features[...].astype(F32)

    bnd = boundaries[...].reshape(1, boundaries.shape[0])
    pos = me * rows + lax.broadcasted_iota(jnp.int32, (rows, 1), 0)
    below = jnp.sum((bnd <= pos).astype(F32), axis=1, keepdims=True).astype(jnp.int32)
    starts = jnp.sum((bnd == pos).astype(F32), axis=1, keepdims=True)
    slot = below - 1 - me * per
    slots = lax.broadcasted_iota(jnp.int32, (rows, 2 * per), 1)
    pick = (jnp.where(slot == slots, 1.0, 0.0) * starts).T.astype(BF16)
    table_rows = table.shape[0]
    entries = lax.broadcasted_iota(jnp.int32, (rows, table_rows), 1)
    spread = jnp.where(slot + TILE == entries, 1.0, 0.0).astype(BF16)

    halo_copy.wait_recv()
    xs[pl.ds(0, TILE), :] = jnp.where(me > 0, halo[...].astype(F32), 0.0)
    mixed = conv_bias[...].reshape(1, channels)
    for k in range(taps):
        mixed = mixed + conv_weight[pl.ds(k, 1), :] * xs[pl.ds(TILE - taps + 1 + k, rows), :]
    mixed = silu(mixed)
    x_in = (mixed[:, :inner].astype(BF16).astype(F32) * in_coef).astype(BF16)
    b32 = mixed[:, inner : inner + state_dim]
    b_part = b32.astype(BF16)
    c_part = mixed[:, inner + state_dim :].astype(BF16)
    state = mm(b32.T.astype(BF16), x_in) * mid_to_end
    for j in range(n):
        sbuf[j] = state[j * piece : (j + 1) * piece].astype(BF16)
    st1 = []
    for off in range(1, n):
        peer = lax.rem(me + off, n)
        c = remote(sbuf.at[peer], rbuf.at[me], st1_send.at[peer], st1_recv.at[me], peer)
        c.start()
        st1.append(c)
    rbuf[me] = sbuf[me]

    prod = lax.dot_general(
        c_part, b_part, (((1,), (1,)), ((), ())), preferred_element_type=F32
    )
    local = mm(jnp.where(causal, prod, 0.0).astype(BF16), x_in)
    loads[0].wait()
    gate = silu(gate_in[...].astype(F32))

    for off in range(1, n):
        src = lax.rem(me + n - off, n)
        remote(dec.at[src], dec.at[src], dec_send.at[src], dec_recv.at[src], src).wait_recv()
    decays = jnp.concatenate([dec[k, 0:1, :] for k in range(n)], axis=0)[:, :heads]
    decays = expand(jnp.exp(decays))
    for off in range(1, n):
        src = lax.rem(me + n - off, n)
        remote(rbuf.at[src], rbuf.at[src], st1_send.at[src], st1_recv.at[src], src).wait_recv()
    before = jnp.zeros((piece, inner), F32)
    for k in range(n):
        obuf[k] = before.astype(BF16)
        before = before * decays[k : k + 1] + rbuf[k].astype(F32)
    st2 = []
    for off in range(1, n):
        peer = lax.rem(me + off, n)
        c = remote(obuf.at[peer], inbuf.at[me], st2_send.at[peer], st2_recv.at[me], peer)
        c.start()
        st2.append(c)
    inbuf[me] = obuf[me]
    for off in range(1, n):
        src = lax.rem(me + n - off, n)
        remote(inbuf.at[src], inbuf.at[src], st2_send.at[src], st2_recv.at[src], src).wait_recv()
    if piece % TILE == 0:
        state_in = inbuf[...].reshape(state_dim, inner)
    else:
        state_in = jnp.concatenate([inbuf[k].astype(F32) for k in range(n)], axis=0).astype(BF16)
    ssm_out = (local + mm(c_part, state_in) * start_to_mid) * out_coef

    gated = ssm_out * gate
    scale = lax.rsqrt(jnp.mean(gated * gated, axis=1, keepdims=True) + EPSILON)
    normed = (gated * scale * gate_gain[...].reshape(1, inner)).astype(BF16)
    loads[1].wait()
    encoded = mm(normed, w_out[...]).astype(BF16)
    enc[...] = encoded
    picked = mm(pick, encoded).astype(BF16)
    upper[...] = picked[per:]
    up_copy = remote(upper, arrived, one_send.at[1], one_recv.at[1], nxt)
    up_copy.start()
    up_copy.wait_recv()
    mine = core * chips + chip
    own_rows = picked[:per].astype(F32) + jnp.where(me > 0, arrived[...].astype(F32), 0.0)
    gath[mine] = own_rows.astype(BF16)

    ag = []
    for off in range(1, chips):
        q = lax.rem(chip + off, chips)
        c = remote(gath.at[mine], gath.at[mine], ag_send.at[q], ag_recv.at[mine], 2 * q + core)
        c.start()
        ag.append(c)
    c = remote(gath.at[mine], gath.at[mine], fwd_send.at[chip], ag_recv.at[mine], partner)
    c.start()
    ag.append(c)
    for off in range(1, chips):
        s = core * chips + lax.rem(chip + chips - off, chips)
        q = lax.rem(chip + chips - off, chips)
        remote(gath.at[s], gath.at[s], ag_send.at[q], ag_recv.at[s], 2 * q + core).wait_recv()
        c = remote(gath.at[s], gath.at[s], fwd_send.at[q], ag_recv.at[s], partner)
        c.start()
        ag.append(c)

    main_width = main_gain.shape[0]
    width = out.shape[1]
    half = chips * per
    gain = main_gain[...].reshape(1, main_width)
    pad = pad_vector[...].astype(F32).reshape(1, main_width - width)
    pad_sum = jnp.sum(pad * pad, axis=1, keepdims=True)
    pad_gain = pad * gain[:, width:]

    def hidden(which):
        rows_in = gath[pl.ds(which * chips, chips)].reshape(half, width).astype(F32)
        mean = (jnp.sum(rows_in * rows_in, axis=1, keepdims=True) + pad_sum) / main_width
        scale = lax.rsqrt(mean + EPSILON)
        nbuf[:, :width] = (rows_in * scale * gain[:, :width]).astype(BF16)
        nbuf[:, width:] = (scale * pad_gain).astype(BF16)
        act = nbuf[...]
        return (silu(mm(act, w_gate[...])) * mm(act, w_up[...])).astype(BF16)

    loads[2].wait()
    loads[3].wait()
    act_own = hidden(core)
    for q in range(chips):
        s = (1 - core) * chips + q
        remote(gath.at[s], gath.at[s], fwd_send.at[q], ag_recv.at[s], partner).wait_recv()
    act_other = hidden(1 - core)
    loads[4].wait()
    part[...] = mm(act_other, w_down[...]).astype(BF16).reshape(chips, per, width)
    rs = []
    for q in range(chips):
        c = remote(part.at[q], pair.at[q], pair_send.at[q], pair_recv.at[q], partner)
        c.start()
        rs.append(c)
    own_part = mm(act_own, w_down[...]).reshape(chips, per, width)
    for q in range(chips):
        remote(part.at[q], pair.at[q], pair_send.at[q], pair_recv.at[q], partner).wait_recv()
    csend[...] = (own_part + pair[...].astype(F32)).astype(BF16)
    for off in range(1, chips):
        q = lax.rem(chip + off, chips)
        c = remote(csend.at[q], crecv.at[chip], chip_send.at[q], chip_recv.at[chip], 2 * q + core)
        c.start()
        rs.append(c)
    result = own_rows + csend[chip].astype(F32)
    for off in range(1, chips):
        q = lax.rem(chip + chips - off, chips)
        remote(csend.at[q], crecv.at[q], chip_send.at[q], chip_recv.at[q], 2 * q + core).wait_recv()
        result = result + crecv[q].astype(F32)
    table[pl.ds(TILE, per), :] = result.astype(BF16)
    fol = remote(
        table.at[pl.ds(TILE, per)],
        table.at[pl.ds(TILE + per, per)],
        one_send.at[2],
        one_recv.at[2],
        prv,
    )
    fol.start()
    ear = remote(
        table.at[pl.ds(per, TILE)],
        table.at[pl.ds(0, TILE)],
        one_send.at[3],
        one_recv.at[3],
        nxt,
    )
    ear.start()
    fol.wait_recv()
    ear.wait_recv()
    expanded = mm(spread, table[...])
    out[...] = (enc[...].astype(F32) + expanded).astype(BF16)

    for c in [halo_copy, up_copy, fol, ear] + dec_copies + st1 + st2 + ag + rs:
        c.wait_send()


def per_device(
    n,
    features,
    gate_in,
    conv_weight,
    conv_bias,
    log_decay,
    step_size,
    gate_gain,
    w_out,
    boundaries,
    pad_vector,
    main_gain,
    w_gate,
    w_up,
    w_down,
):
    rows, channels = features.shape
    inner = gate_in.shape[1]
    width = w_out.shape[1]
    state_dim = (channels - inner) // 2
    piece = state_dim // n
    chips = n // 2
    per = boundaries.shape[0] // n
    half = chips * per
    vmem = pl.BlockSpec(memory_space=pltpu.VMEM)
    hbm = pl.BlockSpec(memory_space=pl.ANY)
    dma = pltpu.SemaphoreType.DMA
    in_hbm = (1, 7, 11, 12, 13)
    return pl.pallas_call(
        functools.partial(kernel, n),
        out_shape=jax.ShapeDtypeStruct((rows, width), BF16),
        in_specs=[hbm if i in in_hbm else vmem for i in range(14)],
        out_specs=vmem,
        scratch_shapes=[
            pltpu.VMEM(gate_in.shape, BF16),
            pltpu.VMEM(w_out.shape, BF16),
            pltpu.VMEM(w_gate.shape, BF16),
            pltpu.VMEM(w_up.shape, BF16),
            pltpu.VMEM(w_down.shape, BF16),
            pltpu.VMEM((TILE, channels), BF16),
            pltpu.VMEM((TILE + rows, channels), F32),
            pltpu.VMEM((n, 8, 128), F32),
            pltpu.VMEM((n, piece, inner), BF16),
            pltpu.VMEM((n, piece, inner), BF16),
            pltpu.VMEM((n, piece, inner), BF16),
            pltpu.VMEM((n, piece, inner), BF16),
            pltpu.VMEM((rows, width), BF16),
            pltpu.VMEM((per, width), BF16),
            pltpu.VMEM((per, width), BF16),
            pltpu.VMEM((n, per, width), BF16),
            pltpu.VMEM((half, main_gain.shape[0]), BF16),
            pltpu.VMEM((chips, per, width), BF16),
            pltpu.VMEM((chips, per, width), BF16),
            pltpu.VMEM((chips, per, width), BF16),
            pltpu.VMEM((chips, per, width), BF16),
            pltpu.VMEM((TILE + 2 * per, width), BF16),
            dma((5,)),
            dma((4,)),
            dma((4,)),
            dma((n,)),
            dma((n,)),
            dma((n,)),
            dma((n,)),
            dma((n,)),
            dma((n,)),
            dma((chips,)),
            dma((chips,)),
            dma((n,)),
            dma((chips,)),
            dma((chips,)),
            dma((chips,)),
            dma((chips,)),
        ],
        compiler_params=pltpu.CompilerParams(collective_id=0, has_side_effects=True),
    )(
        features,
        gate_in,
        conv_weight,
        conv_bias,
        log_decay,
        step_size,
        gate_gain,
        w_out,
        boundaries,
        pad_vector,
        main_gain,
        w_gate,
        w_up,
        w_down,
    )


def solution(mesh):
    in_specs = (
        P(("doc", "seq"), None),
        P(("doc", "seq"), None),
        P(),
        P(),
        P(("doc", "seq"), None),
        P(("doc", "seq"), None),
        P(),
        P(),
        P("doc"),
        P(),
        P(),
        P(None, "seq"),
        P(None, "seq"),
        P("seq", None),
    )
    out_specs = P(("doc", "seq"), None)
    return jax.shard_map(
        functools.partial(per_device, mesh.shape["seq"]),
        mesh=mesh,
        in_specs=in_specs,
        out_specs=out_specs,
        check_vma=False,
    )
```

time: 130 us -> 42.7 us (0.33); the launches traced: 128 us -> 42.5 us
  waiting for transfers between devices: 49.2 us -> 0 us
  Pallas kernels: 0 us -> 37.9 us
  blocking collectives: 22.1 us -> 0 us
  between operations: 14.3 us -> 0.01 us
  starting transfers between devices: 14.1 us -> 0 us
  other arithmetic: 13.8 us -> 0 us
  matrix products: 8.49 us -> 0 us
    pallas_call x0 -> x1, Pallas kernels: none -> 37.9 us  [per_device(): pl.pallas_call(functools.partial(kernel, n), out_shape=jax.ShapeDtypeStru...]
    reduce_scatter x1 -> x0, waiting for transfers between devices: 33.2 us -> none  [main_section(): lax.psum_scatter(jnp.dot(activated, w_down, preferred_element_type=jnp.fl...]
    ppermute x4 -> x0, starting transfers between devices: 14 us -> none  [shifted(): return lax.ppermute(value, axis, pairs)]
    all_gather x1 -> x0, waiting for transfers between devices: 14 us -> none  [prefix(): lax.all_gather(part.astype(kind), axis)]
    all_gather x1 -> x0, blocking collectives: 11.8 us -> none  [main_section(): fragment = lax.all_gather(block_rows, 'seq', axis=0, tiled=True)]
    unnamed x1 -> x0, blocking collectives: 10.3 us -> none
    select_n x8 -> x0, other arithmetic: 8.73 us -> none  [step(): return jax.tree.map(lambda a, b: jnp.where(reached, a, b), new, before)]
    dot_general x9 -> x0, matrix products: 8.49 us -> none  [the longest x1 3.53 us: main_section(): jnp.dot(activated, w_down, preferred_element_type=jnp.float32)]
  transfers between devices with their start and end apart: 6 -> 0, of which waited for: 4 -> 0; matrix products, arithmetic and copies ran while one was open for 5% -> 0% of each run, Pallas kernels for 0% -> 0%
where the time goes in v1:
time: 42.7 us; the launch traced here: 42.5 us
  Pallas kernels  37.9 us (89%)
  local copies, waits for them, and re-layouts  4.51 us (11%)
    pallas_call x1, Pallas kernels, per_device(): pl.pallas_call(functools.partial(kernel, n), out_shape=jax.ShapeDtypeStru...  37.9 us
    unnamed x3, local copies, waits for them, and re-layouts  4.51 us

profile of v1, /device:TPU:1, one launch (start us, length us, event | category | flops | bytes accessed | tf_op | source)
XLA Modules:
  0.0 42.5 jit_solution(14421519892520145321)
XLA Ops:
  0.0 1.4 %copy.15.log_decay = f32[128,16]{1,0:T(8,128)} copy(f32[128,16]{0,1:T(8,128)} %param.18) | data formatting | bytes 16384 | tf_op args[4]
  1.4 1.4 %copy.16.step_size = f32[128,16]{1,0:T(8,128)} copy(f32[128,16]{0,1:T(8,128)} %param.19) | data formatting | bytes 16384 | tf_op args[5]
  2.8 37.9 %shard_map.136 = bf16[128,1024]{1,0:T(8,128)(2,1)} custom-call(bf16[128,1280]{1,0:T(8,128)(2,1)} %features.1, bf16[128,1024]{1,0:T(8,128)(2,1)} %gate_hbm.1, f32[4,1280]{1,0:T(4,128)} %conv_weight.1, f32[1280]{0:T(1024)} %conv_bias.1, f32[128,16]{1,0:T(8,128)} %copy.15.log_decay, f32[128,16]{1,0:T(8,128)} %copy.16.step_size, f32[1024]{0:T(1024)} %gate_gain.1, ...), custom_call_target="tpu_custom_call" | custom-call | tf_op jit(solution)/shard_map/pallas_call | solution.py:369
  40.8 1.7 %copy.18 = bf16[128,1024]{1,0:T(8,128)(2,1)} copy(bf16[128,1024]{1,0:T(8,128)(2,1)} %shard_map.136) | data formatting | bytes 524288

commit v2 on v1

--- a/solution.py
+++ b/solution.py
@@ -23,23 +23,33 @@
 
 def kernel(
     n,
+    per,
+    features_hbm,
+    gate_in_hbm,
+    conv_weight_hbm,
+    conv_bias_hbm,
+    log_decay_hbm,
+    step_size_hbm,
+    gate_gain_hbm,
+    w_out_hbm,
+    boundaries_hbm,
+    pad_vector_hbm,
+    main_gain_hbm,
+    w_gate_hbm,
+    w_up_hbm,
+    w_down_hbm,
+    out,
     features,
-    gate_hbm,
+    gate_in,
     conv_weight,
     conv_bias,
     log_decay,
     step_size,
     gate_gain,
-    w_out_hbm,
+    w_out,
     boundaries,
     pad_vector,
     main_gain,
-    w_gate_hbm,
-    w_up_hbm,
-    w_down_hbm,
-    out,
-    gate_in,
-    w_out,
     w_gate,
     w_up,
     w_down,
@@ -59,6 +69,9 @@
     pair,
     csend,
     crecv,
+    own_part,
+    x_buf,
+    bc_buf,
     table,
     load_sem,
     one_send,
@@ -83,12 +96,11 @@
     partner = chip * 2 + (1 - core)
     nxt, prv = lax.rem(me + 1, n), lax.rem(me + n - 1, n)
     rows, channels = features.shape
-    heads = log_decay.shape[1]
+    heads = log_decay.shape[0]
     inner = gate_in.shape[1]
     head_dim = inner // heads
     state_dim = (channels - inner) // 2
     piece = state_dim // n
-    per = gath.shape[1]
     taps = conv_weight.shape[0]
 
     barrier = pltpu.get_barrier_semaphore()
@@ -100,16 +112,24 @@
             device_id_type=pl.DeviceIdType.MESH,
         )
 
+    order = (
+        (log_decay_hbm, log_decay),
+        (features_hbm, features),
+        (step_size_hbm, step_size),
+        (conv_weight_hbm, conv_weight),
+        (conv_bias_hbm, conv_bias),
+        (boundaries_hbm, boundaries),
+        (gate_in_hbm, gate_in),
+        (gate_gain_hbm, gate_gain),
+        (w_out_hbm, w_out),
+        (pad_vector_hbm, pad_vector),
+        (main_gain_hbm, main_gain),
+        (w_gate_hbm, w_gate),
+        (w_up_hbm, w_up),
+        (w_down_hbm, w_down),
+    )
     loads = []
-    for i, (src, dst) in enumerate(
-        (
-            (gate_hbm, gate_in),
-            (w_out_hbm, w_out),
-            (w_gate_hbm, w_gate),
-            (w_up_hbm, w_up),
-            (w_down_hbm, w_down),
-        )
-    ):
+    for i, (src, dst) in enumerate(order):
         c = pltpu.make_async_copy(src, dst, load_sem.at[i])
         c.start()
         loads.append(c)
@@ -127,9 +147,10 @@
     row_i = lax.broadcasted_iota(jnp.int32, (rows, rows), 0)
     col_i = lax.broadcasted_iota(jnp.int32, (rows, rows), 1)
     causal = row_i >= col_i
+    loads[0].wait()
     cum = jnp.dot(
         causal.astype(F32),
-        log_decay[...],
+        log_decay[...].T,
         preferred_element_type=F32,
         precision=lax.Precision.HIGHEST,
     )
@@ -138,6 +159,8 @@
     dec[me] = jnp.zeros(dec.shape[1:], F32)
     dec[me, :, :heads] = jnp.broadcast_to(total, (dec.shape[1], heads))
 
+    for c in loads[1:6]:
+        c.wait()
     pl.semaphore_wait(barrier, n - 1)
 
     halo_copy = remote(
@@ -160,12 +183,28 @@
         lo = (v - hi.astype(F32)).astype(BF16)
         return mm(hi, onehot) + mm(lo, onehot)
 
-    in_coef = expand(step_size[...] * jnp.exp(mid - cum))
+    in_coef = expand(step_size[...].T * jnp.exp(mid - cum))
     out_coef = expand(jnp.exp(cum - mid))
     mid_to_end = expand(jnp.broadcast_to(jnp.exp(total - mid), (8, heads)))[:1]
     start_to_mid = expand(jnp.broadcast_to(jnp.exp(mid), (8, heads)))[:1]
 
     xs[pl.ds(TILE, rows), :] = features[...].astype(F32)
+
+    def convolved(first, count):
+        mixed = conv_bias[...].reshape(1, channels)
+        for k in range(taps):
+            mixed = mixed + conv_weight[pl.ds(k, 1), :] * xs[
+                pl.ds(TILE - taps + 1 + first + k, count), :
+            ]
+        mixed = silu(mixed)
+        coef = in_coef[first : first + count]
+        x_new = (mixed[:, :inner].astype(BF16).astype(F32) * coef).astype(BF16)
+        x_buf[pl.ds(first, count), :] = x_new
+        bc_buf[pl.ds(first, count), :] = mixed[:, inner:].astype(BF16)
+        b_new = mixed[:, inner : inner + state_dim]
+        return mm(b_new.T.astype(BF16), x_new)
+
+    state = convolved(TILE, rows - TILE)
 
     bnd = boundaries[...].reshape(1, boundaries.shape[0])
     pos = me * rows + lax.broadcasted_iota(jnp.int32, (rows, 1), 0)
@@ -180,15 +219,7 @@
 
     halo_copy.wait_recv()
     xs[pl.ds(0, TILE), :] = jnp.where(me > 0, halo[...].astype(F32), 0.0)
-    mixed = conv_bias[...].reshape(1, channels)
-    for k in range(taps):
-        mixed = mixed + conv_weight[pl.ds(k, 1), :] * xs[pl.ds(TILE - taps + 1 + k, rows), :]
-    mixed = silu(mixed)
-    x_in = (mixed[:, :inner].astype(BF16).astype(F32) * in_coef).astype(BF16)
-    b32 = mixed[:, inner : inner + state_dim]
-    b_part = b32.astype(BF16)
-    c_part = mixed[:, inner + state_dim :].astype(BF16)
-    state = mm(b32.T.astype(BF16), x_in) * mid_to_end
+    state = (state + convolved(0, TILE)) * mid_to_end
     for j in range(n):
         sbuf[j] = state[j * piece : (j + 1) * piece].astype(BF16)
     st1 = []
@@ -199,11 +230,15 @@
         st1.append(c)
     rbuf[me] = sbuf[me]
 
+    x_in = x_buf[...]
+    b_part = bc_buf[:, :state_dim]
+    c_part = bc_buf[:, state_dim:]
     prod = lax.dot_general(
         c_part, b_part, (((1,), (1,)), ((), ())), preferred_element_type=F32
     )
     local = mm(jnp.where(causal, prod, 0.0).astype(BF16), x_in)
-    loads[0].wait()
+    loads[6].wait()
+    loads[7].wait()
     gate = silu(gate_in[...].astype(F32))
 
     for off in range(1, n):
@@ -237,7 +272,7 @@
     gated = ssm_out * gate
     scale = lax.rsqrt(jnp.mean(gated * gated, axis=1, keepdims=True) + EPSILON)
     normed = (gated * scale * gate_gain[...].reshape(1, inner)).astype(BF16)
-    loads[1].wait()
+    loads[8].wait()
     encoded = mm(normed, w_out[...]).astype(BF16)
     enc[...] = encoded
     picked = mm(pick, encoded).astype(BF16)
@@ -266,6 +301,8 @@
         c.start()
         ag.append(c)
 
+    loads[9].wait()
+    loads[10].wait()
     main_width = main_gain.shape[0]
     width = out.shape[1]
     half = chips * per
@@ -283,29 +320,31 @@
         act = nbuf[...]
         return (silu(mm(act, w_gate[...])) * mm(act, w_up[...])).astype(BF16)
 
-    loads[2].wait()
-    loads[3].wait()
+    loads[11].wait()
+    loads[12].wait()
     act_own = hidden(core)
     for q in range(chips):
         s = (1 - core) * chips + q
         remote(gath.at[s], gath.at[s], fwd_send.at[q], ag_recv.at[s], partner).wait_recv()
     act_other = hidden(1 - core)
-    loads[4].wait()
+    loads[13].wait()
     part[...] = mm(act_other, w_down[...]).astype(BF16).reshape(chips, per, width)
     rs = []
-    for q in range(chips):
+    targets = [lax.rem(chip + off, chips) for off in range(1, chips)] + [chip]
+    for q in targets:
         c = remote(part.at[q], pair.at[q], pair_send.at[q], pair_recv.at[q], partner)
         c.start()
         rs.append(c)
-    own_part = mm(act_own, w_down[...]).reshape(chips, per, width)
-    for q in range(chips):
+    own_part[...] = mm(act_own, w_down[...]).reshape(chips, per, width)
+    for i, q in enumerate(targets):
         remote(part.at[q], pair.at[q], pair_send.at[q], pair_recv.at[q], partner).wait_recv()
-    csend[...] = (own_part + pair[...].astype(F32)).astype(BF16)
-    for off in range(1, chips):
-        q = lax.rem(chip + off, chips)
-        c = remote(csend.at[q], crecv.at[chip], chip_send.at[q], chip_recv.at[chip], 2 * q + core)
-        c.start()
-        rs.append(c)
+        csend[q] = (own_part[q] + pair[q].astype(F32)).astype(BF16)
+        if i < chips - 1:
+            c = remote(
+                csend.at[q], crecv.at[chip], chip_send.at[q], chip_recv.at[chip], 2 * q + core
+            )
+            c.start()
+            rs.append(c)
     result = own_rows + csend[chip].astype(F32)
     for off in range(1, chips):
         q = lax.rem(chip + chips - off, chips)
@@ -365,18 +404,29 @@
     vmem = pl.BlockSpec(memory_space=pltpu.VMEM)
     hbm = pl.BlockSpec(memory_space=pl.ANY)
     dma = pltpu.SemaphoreType.DMA
-    in_hbm = (1, 7, 11, 12, 13)
+    args = (
+        features,
+        gate_in,
+        conv_weight,
+        conv_bias,
+        log_decay.T,
+        step_size.T,
+        gate_gain,
+        w_out,
+        boundaries,
+        pad_vector,
+        main_gain,
+        w_gate,
+        w_up,
+        w_down,
+    )
     return pl.pallas_call(
-        functools.partial(kernel, n),
+        functools.partial(kernel, n, per),
         out_shape=jax.ShapeDtypeStruct((rows, width), BF16),
-        in_specs=[hbm if i in in_hbm else vmem for i in range(14)],
+        in_specs=[hbm] * len(args),
         out_specs=vmem,
         scratch_shapes=[
-            pltpu.VMEM(gate_in.shape, BF16),
-            pltpu.VMEM(w_out.shape, BF16),
-            pltpu.VMEM(w_gate.shape, BF16),
-            pltpu.VMEM(w_up.shape, BF16),
-            pltpu.VMEM(w_down.shape, BF16),
+            *[pltpu.VMEM(a.shape, a.dtype) for a in args],
             pltpu.VMEM((TILE, channels), BF16),
             pltpu.VMEM((TILE + rows, channels), F32),
             pltpu.VMEM((n, 8, 128), F32),
@@ -393,8 +443,11 @@
             pltpu.VMEM((chips, per, width), BF16),
             pltpu.VMEM((chips, per, width), BF16),
             pltpu.VMEM((chips, per, width), BF16),
+            pltpu.VMEM((chips, per, width), F32),
+            pltpu.VMEM((rows, inner), BF16),
+            pltpu.VMEM((rows, 2 * state_dim), BF16),
             pltpu.VMEM((TILE + 2 * per, width), BF16),
-            dma((5,)),
+            dma((len(args),)),
             dma((4,)),
             dma((4,)),
             dma((n,)),
@@ -412,22 +465,7 @@
             dma((chips,)),
         ],
         compiler_params=pltpu.CompilerParams(collective_id=0, has_side_effects=True),
-    )(
-        features,
-        gate_in,
-        conv_weight,
-        conv_bias,
-        log_decay,
-        step_size,
-        gate_gain,
-        w_out,
-        boundaries,
-        pad_vector,
-        main_gain,
-        w_gate,
-        w_up,
-        w_down,
-    )
+    )(*args)
 
 
 def solution(mesh):

time: 42.7 us -> 38.3 us (0.90)
  local copies, waits for them, and re-layouts: 4.51 us -> 1.67 us
  Pallas kernels: 37.9 us -> 36.4 us
    unnamed x3 -> x1, local copies, waits for them, and re-layouts: 4.51 us -> 1.67 us
    pallas_call x1, Pallas kernels: 37.9 us -> 36.4 us  [per_device(): pl.pallas_call(functools.partial(kernel, n, per), out_shape=jax.ShapeDtyp...]
where the time goes in v2:
time: 38.3 us; the launch traced here: 38.1 us
  Pallas kernels  36.4 us (95%)
  local copies, waits for them, and re-layouts  1.67 us (4%)
    pallas_call x1, Pallas kernels, per_device(): pl.pallas_call(functools.partial(kernel, n, per), out_shape=jax.ShapeDtyp...  36.4 us
    unnamed x1, local copies, waits for them, and re-layouts  1.67 us

profile of v2, /device:TPU:1, one launch (start us, length us, event | category | flops | bytes accessed | tf_op | source)
XLA Modules:
  0.0 38.1 jit_solution(17639514337018520827)
XLA Ops:
  0.0 36.4 %shard_map.136 = bf16[128,1024]{1,0:T(8,128)(2,1)} custom-call(bf16[128,1280]{1,0:T(8,128)(2,1)} %features_hbm.1, bf16[128,1024]{1,0:T(8,128)(2,1)} %gate_in_hbm.1, f32[4,1280]{1,0:T(4,128)} %conv_weight_hbm.1, f32[1280]{0:T(1024)} %conv_bias_hbm.1, f32[16,128]{1,0:T(8,128)} %bitcast.2, f32[16,128]{1,0:T(8,128)} %bitcast.3, f32[1024]{0:T(1024)} %gate_gain_hbm.1, ...), custom_call_target="tpu_custom_call" | custom-call | tf_op jit(solution)/shard_map/pallas_call | solution.py:423
  36.4 1.7 %copy.16 = bf16[128,1024]{1,0:T(8,128)(2,1)} copy(bf16[128,1024]{1,0:T(8,128)(2,1)} %shard_map.136) | data formatting | bytes 524288

commit v3 on v2

--- a/solution.py
+++ b/solution.py
@@ -70,6 +70,8 @@
     csend,
     crecv,
     own_part,
+    ubuf,
+    hbuf,
     x_buf,
     bc_buf,
     table,
@@ -89,6 +91,9 @@
     pair_recv,
     chip_send,
     chip_recv,
+    u_send,
+    uf_send,
+    u_recv,
 ):
     me = lax.axis_index("seq")
     chips = n // 2
@@ -103,6 +108,7 @@
     piece = state_dim // n
     taps = conv_weight.shape[0]
 
+    arrived[...] = jnp.zeros(arrived.shape, BF16)
     barrier = pltpu.get_barrier_semaphore()
     for off in range(1, n):
         pl.semaphore_signal(
@@ -277,29 +283,58 @@
     enc[...] = encoded
     picked = mm(pick, encoded).astype(BF16)
     upper[...] = picked[per:]
-    up_copy = remote(upper, arrived, one_send.at[1], one_recv.at[1], nxt)
-    up_copy.start()
-    up_copy.wait_recv()
     mine = core * chips + chip
-    own_rows = picked[:per].astype(F32) + jnp.where(me > 0, arrived[...].astype(F32), 0.0)
-    gath[mine] = own_rows.astype(BF16)
+    others = [lax.rem(chip + off, chips) for off in range(1, chips)]
+    sources = [lax.rem(chip + chips - off, chips) for off in range(1, chips)]
+
+    up_copy = remote(upper, arrived, one_send.at[1], one_recv.at[1], partner)
+    u_copies = [
+        remote(upper, ubuf.at[chip], u_send.at[q], u_recv.at[chip], 2 * q + core) for q in others
+    ]
+    u_copies.append(remote(upper, ubuf.at[chip], uf_send.at[chip], u_recv.at[chip], partner))
+
+    @pl.when(core == 0)
+    def _():
+        up_copy.start()
+
+    @pl.when(core == 1)
+    def _():
+        for c in u_copies:
+            c.start()
+        ubuf[chip] = upper[...]
+        up_copy.wait_recv()
+
+    gath[mine] = (
+        picked[:per].astype(F32) + jnp.where(core == 1, arrived[...].astype(F32), 0.0)
+    ).astype(BF16)
 
     ag = []
-    for off in range(1, chips):
-        q = lax.rem(chip + off, chips)
+    for q in others:
         c = remote(gath.at[mine], gath.at[mine], ag_send.at[q], ag_recv.at[mine], 2 * q + core)
         c.start()
         ag.append(c)
     c = remote(gath.at[mine], gath.at[mine], fwd_send.at[chip], ag_recv.at[mine], partner)
     c.start()
     ag.append(c)
-    for off in range(1, chips):
-        s = core * chips + lax.rem(chip + chips - off, chips)
-        q = lax.rem(chip + chips - off, chips)
+    u_forwards = [remote(ubuf.at[q], ubuf.at[q], uf_send.at[q], u_recv.at[q], partner) for q in sources]
+
+    @pl.when(core == 1)
+    def _():
+        for c in u_forwards:
+            c.wait_recv()
+            c.start()
+
+    for q in sources:
+        s = core * chips + q
         remote(gath.at[s], gath.at[s], ag_send.at[q], ag_recv.at[s], 2 * q + core).wait_recv()
         c = remote(gath.at[s], gath.at[s], fwd_send.at[q], ag_recv.at[s], partner)
         c.start()
         ag.append(c)
+
+    def await_parity(which):
+        for q in range(chips):
+            s = which * chips + q
+            remote(gath.at[s], gath.at[s], fwd_send.at[q], ag_recv.at[s], partner).wait_recv()
 
     loads[9].wait()
     loads[10].wait()
@@ -313,29 +348,46 @@
 
     def hidden(which):
         rows_in = gath[pl.ds(which * chips, chips)].reshape(half, width).astype(F32)
+        if which == 0:
+            spill = ubuf[pl.ds(0, chips - 1)].reshape(half - per, width).astype(F32)
+            rows_in = rows_in + jnp.concatenate([jnp.zeros((per, width), F32), spill], axis=0)
         mean = (jnp.sum(rows_in * rows_in, axis=1, keepdims=True) + pad_sum) / main_width
         scale = lax.rsqrt(mean + EPSILON)
         nbuf[:, :width] = (rows_in * scale * gain[:, :width]).astype(BF16)
         nbuf[:, width:] = (scale * pad_gain).astype(BF16)
         act = nbuf[...]
-        return (silu(mm(act, w_gate[...])) * mm(act, w_up[...])).astype(BF16)
+        hbuf[which] = (silu(mm(act, w_gate[...])) * mm(act, w_up[...])).astype(BF16)
 
     loads[11].wait()
     loads[12].wait()
-    act_own = hidden(core)
-    for q in range(chips):
-        s = (1 - core) * chips + q
-        remote(gath.at[s], gath.at[s], fwd_send.at[q], ag_recv.at[s], partner).wait_recv()
-    act_other = hidden(1 - core)
+
+    @pl.when(core == 0)
+    def _():
+        await_parity(1)
+
+    hidden(1)
+
+    @pl.when(core == 1)
+    def _():
+        await_parity(0)
+
+    @pl.when(core == 0)
+    def _():
+        for q in range(chips):
+            remote(ubuf.at[q], ubuf.at[q], uf_send.at[q], u_recv.at[q], partner).wait_recv()
+
+    hidden(0)
+    before_me = ubuf[lax.rem(chip + chips - 1, chips)].astype(F32)
+    own_rows = gath[mine].astype(F32) + jnp.where((core == 0) & (chip > 0), before_me, 0.0)
     loads[13].wait()
-    part[...] = mm(act_other, w_down[...]).astype(BF16).reshape(chips, per, width)
+    part[...] = mm(hbuf[1 - core], w_down[...]).astype(BF16).reshape(chips, per, width)
     rs = []
     targets = [lax.rem(chip + off, chips) for off in range(1, chips)] + [chip]
     for q in targets:
         c = remote(part.at[q], pair.at[q], pair_send.at[q], pair_recv.at[q], partner)
         c.start()
         rs.append(c)
-    own_part[...] = mm(act_own, w_down[...]).reshape(chips, per, width)
+    own_part[...] = mm(hbuf[core], w_down[...]).reshape(chips, per, width)
     for i, q in enumerate(targets):
         remote(part.at[q], pair.at[q], pair_send.at[q], pair_recv.at[q], partner).wait_recv()
         csend[q] = (own_part[q] + pair[q].astype(F32)).astype(BF16)
@@ -372,8 +424,17 @@
     expanded = mm(spread, table[...])
     out[...] = (enc[...].astype(F32) + expanded).astype(BF16)
 
-    for c in [halo_copy, up_copy, fol, ear] + dec_copies + st1 + st2 + ag + rs:
+    for c in [halo_copy, fol, ear] + dec_copies + st1 + st2 + ag + rs:
         c.wait_send()
+
+    @pl.when(core == 0)
+    def _():
+        up_copy.wait_send()
+
+    @pl.when(core == 1)
+    def _():
+        for c in u_copies + u_forwards:
+            c.wait_send()
 
 
 def per_device(
@@ -422,7 +483,7 @@
     )
     return pl.pallas_call(
         functools.partial(kernel, n, per),
-        out_shape=jax.ShapeDtypeStruct((rows, width), BF16),
+        out_shape=pltpu.VMEM((rows, width), BF16),
         in_specs=[hbm] * len(args),
         out_specs=vmem,
         scratch_shapes=[
@@ -444,6 +505,8 @@
             pltpu.VMEM((chips, per, width), BF16),
             pltpu.VMEM((chips, per, width), BF16),
             pltpu.VMEM((chips, per, width), F32),
+            pltpu.VMEM((chips, per, width), BF16),
+            pltpu.VMEM((2, half, w_down.shape[0]), BF16),
             pltpu.VMEM((rows, inner), BF16),
             pltpu.VMEM((rows, 2 * state_dim), BF16),
             pltpu.VMEM((TILE + 2 * per, width), BF16),
@@ -459,6 +522,9 @@
             dma((chips,)),
             dma((chips,)),
             dma((n,)),
+            dma((chips,)),
+            dma((chips,)),
+            dma((chips,)),
             dma((chips,)),
             dma((chips,)),
             dma((chips,)),

time: 38.3 us -> 35.9 us (0.937)
  Pallas kernels: 36.4 us -> 35 us
  local copies, waits for them, and re-layouts: 1.67 us -> 0.71 us
    pallas_call x1, Pallas kernels: 36.4 us -> 35 us  [per_device(): pl.pallas_call(functools.partial(kernel, n, per), out_shape=pltpu.VMEM((r...]
    unnamed x1, local copies, waits for them, and re-layouts: 1.67 us -> 0.71 us
where the time goes in v3:
time: 35.9 us; the launch traced here: 35.7 us
  Pallas kernels  35 us (97%)
  local copies, waits for them, and re-layouts  0.71 us (2%)
    pallas_call x1, Pallas kernels, per_device(): pl.pallas_call(functools.partial(kernel, n, per), out_shape=pltpu.VMEM((r...  35 us

profile of v3, /device:TPU:1, one launch (start us, length us, event | category | flops | bytes accessed | tf_op | source)
XLA Modules:
  0.0 35.7 jit_solution(5000230339324119237)
XLA Ops:
  0.0 35.0 %shard_map.136 = bf16[128,1024]{1,0:T(8,128)(2,1)S(1)} custom-call(bf16[128,1280]{1,0:T(8,128)(2,1)} %features_hbm.1, bf16[128,1024]{1,0:T(8,128)(2,1)} %gate_in_hbm.1, f32[4,1280]{1,0:T(4,128)} %conv_weight_hbm.1, f32[1280]{0:T(1024)} %conv_bias_hbm.1, f32[16,128]{1,0:T(8,128)} %bitcast.2, f32[16,128]{1,0:T(8,128)} %bitcast.3, f32[1024]{0:T(1024)} %gate_gain_hbm.1, ...), custom_call_target="tpu_custom_call" | custom-call | tf_op jit(solution)/shard_map/pallas_call | solution.py:484
  35.0 0.7 %copy.16 = bf16[128,1024]{1,0:T(8,128)(2,1)} copy(bf16[128,1024]{1,0:T(8,128)(2,1)S(1)} %shard_map.136) | data formatting | bytes 524288
